TPU v7x, 256 devices: a whole 4x4x8 slice. The times are simulated.
256 devices in a mesh: row: 16 (over z, core), col: 16 (over y, x).
Axes of the slice: x: 4, y: 4, z: 8, core: 2. Of those that a mesh axis runs over, the one named last changes fastest.
Arguments:
- right_sides: float32 [4, 1024, 4096], P(None, 'row', 'col'), may hold values from -6 to 6
- low_left: bfloat16 [6, 4096, 128], P(None, 'col'), may hold values from -0.25 to 0.25
- low_right: bfloat16 [6, 4096, 128], P(None, 'col'), may hold values from -0.09375 to 0.09375
- up_left: bfloat16 [6, 4096, 128], P(None, 'col'), may hold values from -0.25 to 0.25
- up_right: bfloat16 [6, 4096, 128], P(None, 'col'), may hold values from -0.09375 to 0.09375
- low_ranks: int32 [6], replicated, may hold values from 1 to 4
- up_ranks: int32 [6], replicated, may hold values from 1 to 4
- inv_lower: bfloat16 [4, 4096, 4096], P(None, 'col', 'row'), may hold values from -0.09375 to 0.09375
- inv_upper: bfloat16 [4, 4096, 4096], P(None, 'col', 'row'), may hold values from -0.09375 to 0.09375
Outputs:
- solution: float32 [4, 1024, 4096], P(None, 'row', 'col')
Inputs may be any that keep to these rules, and one draw needn't show every extreme that they name: `low_ranks`: factor columns beyond 32 times this value are padding with arbitrary values and must be masked out. `up_ranks`: factor columns beyond 32 times this value are padding with arbitrary values and must be masked out.
All inputs are finite; a program needn't handle non-finite values.
Results may differ from a plain program's by a relative error of at most 0.03.
Values may be sent and summed in bfloat16 or wider, within the bound.
No kernel may reach another device: no remote copies, remote signals or barrier semaphores. Data moves between devices by JAX's collectives and lax.ppermute only.
A program may use at most 64 MiB of HBM per device.

v0:
```python
import jax
import jax.numpy as jnp
import numpy as np
from jax import lax
from jax.sharding import PartitionSpec as P

RBLK = 32


def laid_out(parts, dim):
    parts = jnp.moveaxis(parts, 0, dim)
    lengths = parts.shape
    return parts.reshape(*lengths[:dim], lengths[dim] * lengths[dim + 1], *lengths[dim + 2 :])


def from_everyone(value, axis):
    length = lax.axis_size(axis)
    return lax.all_to_all(
        jnp.broadcast_to(value[None], (length, *value.shape)), axis, 0, 0, tiled=True
    )


def gathered_copies(value, axis, dim):
    return laid_out(from_everyone(value, axis), dim)


def of_everyone(value, axis):
    everything = from_everyone(value, axis)
    return jnp.sum(everything.astype(jnp.float32), axis=0)


def rank_mask(ranks, pair_index, rank_cols):
    columns = jnp.arange(rank_cols, dtype=jnp.int32)
    return (columns[None, :] < RBLK * ranks[pair_index][:, None]).astype(jnp.float32)


def times_inverse(block, inverse):
    return lax.dot_general(
        block, inverse, (((1,), (1,)), ((), ())), preferred_element_type=jnp.float32
    )


def fold_columns(whole, piece):
    return times_inverse(whole, piece)


def shards(
    right_sides, low_left, low_right, up_left, up_right, low_ranks, up_ranks, inv_lower, inv_upper
):
    tile_count = right_sides.shape[0]
    rank_cols = low_left.shape[2]
    residual = right_sides
    forward = []
    for section in range(tile_count):
        rounded = residual[section].astype(jnp.bfloat16)
        whole = gathered_copies(rounded, "col", 1)
        solved = fold_columns(whole, lax.all_gather(inv_lower[section], "row", axis=1, tiled=True))
        forward.append(solved)
        if section + 1 < tile_count:
            pair_index = np.array(
                [tile * (tile - 1) // 2 + section for tile in range(section + 1, tile_count)],
                dtype=np.int32,
            )
            projections = jnp.einsum(
                "nw,mwr->mnr",
                solved.astype(jnp.bfloat16),
                low_right[pair_index],
                preferred_element_type=jnp.float32,
            )
            summed = of_everyone(projections.astype(jnp.bfloat16), "col").astype(jnp.float32)
            masked = (summed * rank_mask(low_ranks, pair_index, rank_cols)[:, None, :]).astype(
                jnp.bfloat16
            )
            update = jnp.einsum(
                "mnr,mwr->mnw", masked, low_left[pair_index], preferred_element_type=jnp.float32
            )
            residual = residual.at[section + 1 :].add(-update)
    state = jnp.stack(forward)
    solutions = [None] * tile_count
    for section in range(tile_count - 1, -1, -1):
        rounded = state[section].astype(jnp.bfloat16)
        whole = gathered_copies(rounded, "col", 1)
        solved = fold_columns(whole, lax.all_gather(inv_upper[section], "row", axis=1, tiled=True))
        solutions[section] = solved
        if section > 0:
            pair_index = np.array(
                [section * (section - 1) // 2 + tile for tile in range(section)], dtype=np.int32
            )
            projections = jnp.einsum(
                "nw,mwr->mnr",
                solved.astype(jnp.bfloat16),
                up_right[pair_index],
                preferred_element_type=jnp.float32,
            )
            summed = of_everyone(projections.astype(jnp.bfloat16), "col").astype(jnp.float32)
            masked = (summed * rank_mask(up_ranks, pair_index, rank_cols)[:, None, :]).astype(
                jnp.bfloat16
            )
            update = jnp.einsum(
                "mnr,mwr->mnw", masked, up_left[pair_index], preferred_element_type=jnp.float32
            )
            state = state.at[:section].add(-update)
    return jnp.stack(solutions)


def solution(mesh):
    in_specs = (
        P(None, "row", "col"),
        P(None, "col", None),
        P(None, "col", None),
        P(None, "col", None),
        P(None, "col", None),
        P(),
        P(),
        P(None, "col", "row"),
        P(None, "col", "row"),
    )
    out_specs = P(None, "row", "col")
    return jax.shard_map(shards, mesh=mesh, in_specs=in_specs, out_specs=out_specs, check_vma=False)
```

profile of v0, /device:TPU:1, one launch (start us, length us, event | category | flops | bytes accessed | tf_op | source)
XLA Modules:
  0.0 357.1 jit_solution(16431836217036689485)
XLA Ops:
  13.4 7.6 %all-to-all-start = ((bf16[16,64,256]{2,1,0:T(8,128)(2,1)}), bf16[16,64,256]{2,1,0:T(8,128)(2,1)S(1)}, u32[]{:S(2)}, u32[]{:S(2)}) async-start(bf16[16,64,256]{2,1,0:T(8,128)(2,1)} %broadcast_in_dim.83), calls=%async_computation | async-start | bytes 1048576 | tf_op jit(solution)/shard_map/all_to_all | solution.py:18
  21.6 9.9 %all-to-all-done = bf16[16,64,256]{2,1,0:T(8,128)(2,1)S(1)} async-done(((bf16[16,64,256]{2,1,0:T(8,128)(2,1)}), bf16[16,64,256]{2,1,0:T(8,128)(2,1)S(1)}, u32[]{:S(2)}, u32[]{:S(2)}) %all-to-all-start) | async-done | bytes 524320 | tf_op jit(solution)/shard_map/all_to_all | solution.py:18
  31.6 22.7 %all-gather.17.cloned.1.call-done = bf16[1,256,4096]{2,1,0:T(8,128)(2,1)} async-done(((bf16[1,256,256]{2,1,0:T(8,128)(2,1)}), bf16[1,256,4096]{2,1,0:T(8,128)(2,1)}) %all-gather.17.cloned.1.call-update) | async-done | bytes 2097168 | tf_op jit(solution)/shard_map/all_gather | solution.py:57
  57.9 6.5 %all-to-all-start.1 = ((bf16[16,3,64,128]{3,2,1,0:T(8,128)(2,1)}), bf16[16,3,64,128]{3,2,1,0:T(8,128)(2,1)S(1)}, u32[]{:S(2)}, u32[]{:S(2)}) async-start(bf16[16,3,64,128]{3,2,1,0:T(8,128)(2,1)} %broadcast_in_dim.85), calls=%async_computation.1 | async-start | bytes 1572864 | tf_op jit(solution)/shard_map/all_to_all | solution.py:18
  66.4 11.7 %all-to-all-done.1 = bf16[16,3,64,128]{3,2,1,0:T(8,128)(2,1)S(1)} async-done(((bf16[16,3,64,128]{3,2,1,0:T(8,128)(2,1)}), bf16[16,3,64,128]{3,2,1,0:T(8,128)(2,1)S(1)}, u32[]{:S(2)}, u32[]{:S(2)}) %all-to-all-start.1) | async-done | bytes 786464 | tf_op jit(solution)/shard_map/all_to_all | solution.py:18
  83.5 9.5 %all-to-all-done.2 = bf16[16,64,256]{2,1,0:T(8,128)(2,1)S(1)} async-done(((bf16[16,64,256]{2,1,0:T(8,128)(2,1)}), bf16[16,64,256]{2,1,0:T(8,128)(2,1)S(1)}, u32[]{:S(2)}, u32[]{:S(2)}) %all-to-all-start.2) | async-done | bytes 524320 | tf_op jit(solution)/shard_map/all_to_all | solution.py:18
  107.5 9.5 %all-to-all-done.3 = bf16[16,2,64,128]{3,2,1,0:T(8,128)(2,1)S(1)} async-done(((bf16[16,2,64,128]{3,2,1,0:T(8,128)(2,1)}), bf16[16,2,64,128]{3,2,1,0:T(8,128)(2,1)S(1)}, u32[]{:S(2)}, u32[]{:S(2)}) %all-to-all-start.3) | async-done | bytes 524320 | tf_op jit(solution)/shard_map/all_to_all | solution.py:18
  122.4 9.3 %all-to-all-done.4 = bf16[16,64,256]{2,1,0:T(8,128)(2,1)S(1)} async-done(((bf16[16,64,256]{2,1,0:T(8,128)(2,1)}), bf16[16,64,256]{2,1,0:T(8,128)(2,1)S(1)}, u32[]{:S(2)}, u32[]{:S(2)}) %all-to-all-start.4) | async-done | bytes 524320 | tf_op jit(solution)/shard_map/all_to_all | solution.py:18
  141.3 6.5 %all-to-all-start.5 = ((bf16[16,1,64,128]{3,2,1,0:T(8,128)(2,1)}), bf16[16,1,64,128]{3,2,1,0:T(8,128)(2,1)S(1)}, u32[]{:S(2)}, u32[]{:S(2)}) async-start(bf16[16,1,64,128]{3,2,1,0:T(8,128)(2,1)} %broadcast_in_dim.191), calls=%async_computation.5 | async-start | bytes 524288 | tf_op jit(solution)/shard_map/all_to_all | solution.py:18
  149.0 7.1 %all-to-all-done.5 = bf16[16,1,64,128]{3,2,1,0:T(8,128)(2,1)S(1)} async-done(((bf16[16,1,64,128]{3,2,1,0:T(8,128)(2,1)}), bf16[16,1,64,128]{3,2,1,0:T(8,128)(2,1)S(1)}, u32[]{:S(2)}, u32[]{:S(2)}) %all-to-all-start.5) | async-done | bytes 262176 | tf_op jit(solution)/shard_map/all_to_all | solution.py:18
  156.3 12.8 %all_to_all.70 = bf16[16,64,256]{2,1,0:T(8,128)(2,1)S(1)} all-to-all(bf16[16,64,256]{2,1,0:T(8,128)(2,1)S(1)} %broadcast_in_dim.195), channel_id=1, replica_groups=mesh['row'=16,'col'=16] {'col'}, dimensions={0} | all-to-all | bytes 1048576 | tf_op jit(solution)/shard_map/all_to_all | solution.py:18
  169.2 10.6 %all-gather.23.cloned.1.call-done = bf16[1,256,4096]{2,1,0:T(8,128)(2,1)} async-done(((bf16[1,256,256]{2,1,0:T(8,128)(2,1)}), bf16[1,256,4096]{2,1,0:T(8,128)(2,1)}) %all-gather.23.cloned.1.call-update) | async-done | bytes 2097168 | tf_op jit(solution)/shard_map/all_gather | solution.py:57
  190.2 10.2 %all-to-all-done.7 = bf16[16,64,256]{2,1,0:T(8,128)(2,1)S(1)} async-done(((bf16[16,64,256]{2,1,0:T(8,128)(2,1)}), bf16[16,64,256]{2,1,0:T(8,128)(2,1)S(1)}, u32[]{:S(2)}, u32[]{:S(2)}) %all-to-all-start.7) | async-done | bytes 524320 | tf_op jit(solution)/shard_map/all_to_all | solution.py:18
  200.5 21.2 %all-gather.25.cloned.1.call-done = bf16[1,256,4096]{2,1,0:T(8,128)(2,1)} async-done(((bf16[1,256,256]{2,1,0:T(8,128)(2,1)}), bf16[1,256,4096]{2,1,0:T(8,128)(2,1)}) %all-gather.25.cloned.1.call-update) | async-done | bytes 2097168 | tf_op jit(solution)/shard_map/all_gather | solution.py:83
  225.3 6.5 %all-to-all-start.8 = ((bf16[16,3,64,128]{3,2,1,0:T(8,128)(2,1)}), bf16[16,3,64,128]{3,2,1,0:T(8,128)(2,1)S(1)}, u32[]{:S(2)}, u32[]{:S(2)}) async-start(bf16[16,3,64,128]{3,2,1,0:T(8,128)(2,1)} %broadcast_in_dim.197), calls=%async_computation.8 | async-start | bytes 1572864 | tf_op jit(solution)/shard_map/all_to_all | solution.py:18
  233.2 12.3 %all-to-all-done.8 = bf16[16,3,64,128]{3,2,1,0:T(8,128)(2,1)S(1)} async-done(((bf16[16,3,64,128]{3,2,1,0:T(8,128)(2,1)}), bf16[16,3,64,128]{3,2,1,0:T(8,128)(2,1)S(1)}, u32[]{:S(2)}, u32[]{:S(2)}) %all-to-all-start.8) | async-done | bytes 786464 | tf_op jit(solution)/shard_map/all_to_all | solution.py:18
  251.6 8.8 %all-to-all-done.9 = bf16[16,64,256]{2,1,0:T(8,128)(2,1)S(1)} async-done(((bf16[16,64,256]{2,1,0:T(8,128)(2,1)}), bf16[16,64,256]{2,1,0:T(8,128)(2,1)S(1)}, u32[]{:S(2)}, u32[]{:S(2)}) %all-to-all-start.9) | async-done | bytes 524320 | tf_op jit(solution)/shard_map/all_to_all | solution.py:18
  266.8 6.5 %all-to-all-start.10 = ((bf16[16,2,64,128]{3,2,1,0:T(8,128)(2,1)}), bf16[16,2,64,128]{3,2,1,0:T(8,128)(2,1)S(1)}, u32[]{:S(2)}, u32[]{:S(2)}) async-start(bf16[16,2,64,128]{3,2,1,0:T(8,128)(2,1)} %broadcast_in_dim.203), calls=%async_computation.10 | async-start | bytes 1048576 | tf_op jit(solution)/shard_map/all_to_all | solution.py:18
  274.7 9.5 %all-to-all-done.10 = bf16[16,2,64,128]{3,2,1,0:T(8,128)(2,1)S(1)} async-done(((bf16[16,2,64,128]{3,2,1,0:T(8,128)(2,1)}), bf16[16,2,64,128]{3,2,1,0:T(8,128)(2,1)S(1)}, u32[]{:S(2)}, u32[]{:S(2)}) %all-to-all-start.10) | async-done | bytes 524320 | tf_op jit(solution)/shard_map/all_to_all | solution.py:18
  284.5 13.4 %all_to_all.71 = bf16[16,64,256]{2,1,0:T(8,128)(2,1)S(1)} all-to-all(bf16[16,64,256]{2,1,0:T(8,128)(2,1)S(1)} %broadcast_in_dim.208), channel_id=1, replica_groups=mesh['row'=16,'col'=16] {'col'}, dimensions={0} | all-to-all | bytes 1048576 | tf_op jit(solution)/shard_map/all_to_all | solution.py:18
  297.9 7.4 %all-gather.29.cloned.1.call-done = bf16[1,256,4096]{2,1,0:T(8,128)(2,1)} async-done(((bf16[1,256,256]{2,1,0:T(8,128)(2,1)}), bf16[1,256,4096]{2,1,0:T(8,128)(2,1)}) %all-gather.29.cloned.1.call-update) | async-done | bytes 2097168 | tf_op jit(solution)/shard_map/all_gather | solution.py:83
  315.1 8.2 %all-to-all-done.12 = bf16[16,1,64,128]{3,2,1,0:T(8,128)(2,1)S(1)} async-done(((bf16[16,1,64,128]{3,2,1,0:T(8,128)(2,1)}), bf16[16,1,64,128]{3,2,1,0:T(8,128)(2,1)S(1)}, u32[]{:S(2)}, u32[]{:S(2)}) %all-to-all-start.12) | async-done | bytes 262176 | tf_op jit(solution)/shard_map/all_to_all | solution.py:18
  323.5 12.8 %all_to_all.72 = bf16[16,64,256]{2,1,0:T(8,128)(2,1)S(1)} all-to-all(bf16[16,64,256]{2,1,0:T(8,128)(2,1)S(1)} %broadcast_in_dim.214), channel_id=1, replica_groups=mesh['row'=16,'col'=16] {'col'}, dimensions={0} | all-to-all | bytes 1048576 | tf_op jit(solution)/shard_map/all_to_all | solution.py:18
  336.4 10.8 %all-gather.31.cloned.1.call-done = bf16[1,256,4096]{2,1,0:T(8,128)(2,1)} async-done(((bf16[1,256,256]{2,1,0:T(8,128)(2,1)}), bf16[1,256,4096]{2,1,0:T(8,128)(2,1)}) %all-gather.31.cloned.1.call-update) | async-done | bytes 2097168 | tf_op jit(solution)/shard_map/all_gather | solution.py:83
  (130 shorter events, 91.2 us)
Async XLA Ops:
  6.5 14.5 %copy-start.10 = (s32[3]{0:T(128)S(1)}, s32[3]{0:T(128)}, u32[]{:S(2)}) copy-start(s32[3]{0:T(128)} %constant.313) | copy-start | bytes 40
  6.5 14.5 %copy-start.2 = (bf16[6,256,128]{2,1,0:T(8,128)(2,1)S(1)}, bf16[6,256,128]{2,1,0:T(8,128)(2,1)}, u32[]{:S(2)}) copy-start(bf16[6,256,128]{2,1,0:T(8,128)(2,1)} %param.47) | copy-start | bytes 1179652
  6.5 47.7 %all-gather.17.cloned.1.call-start = ((), (), s32[]{:S(2)}) async-start(), calls=%async_computation.14 | async-start | bytes 2228224 | tf_op jit(solution)/shard_map/all_gather | solution.py:57
  8.5 87.7 %all-gather.19.cloned.1.call-start = ((), (), s32[]{:S(2)}) async-start(), calls=%async_computation.15 | async-start | bytes 2228224 | tf_op jit(solution)/shard_map/all_gather | solution.py:57
  9.3 128.8 %all-gather.21.cloned.1.call-start = ((), (), s32[]{:S(2)}) async-start(), calls=%async_computation.16 | async-start | bytes 2228224 | tf_op jit(solution)/shard_map/all_gather | solution.py:57
  10.0 169.8 %all-gather.23.cloned.1.call-start = ((), (), s32[]{:S(2)}) async-start(), calls=%async_computation.17 | async-start | bytes 2228224 | tf_op jit(solution)/shard_map/all_gather | solution.py:57
  10.6 211.0 %all-gather.25.cloned.1.call-start = ((), (), s32[]{:S(2)}) async-start(), calls=%async_computation.18 | async-start | bytes 2228224 | tf_op jit(solution)/shard_map/all_gather | solution.py:83
  13.4 18.1 %all-to-all-start = ((bf16[16,64,256]{2,1,0:T(8,128)(2,1)}), bf16[16,64,256]{2,1,0:T(8,128)(2,1)S(1)}, u32[]{:S(2)}, u32[]{:S(2)}) async-start(bf16[16,64,256]{2,1,0:T(8,128)(2,1)} %broadcast_in_dim.83), calls=%async_computation | async-start | bytes 1048576 | tf_op jit(solution)/shard_map/all_to_all | solution.py:18
  57.9 20.2 %all-to-all-start.1 = ((bf16[16,3,64,128]{3,2,1,0:T(8,128)(2,1)}), bf16[16,3,64,128]{3,2,1,0:T(8,128)(2,1)S(1)}, u32[]{:S(2)}, u32[]{:S(2)}) async-start(bf16[16,3,64,128]{3,2,1,0:T(8,128)(2,1)} %broadcast_in_dim.85), calls=%async_computation.1 | async-start | bytes 1572864 | tf_op jit(solution)/shard_map/all_to_all | solution.py:18
  64.4 198.9 %all-gather.27.cloned.1.call-start = ((), (), s32[]{:S(2)}) async-start(), calls=%async_computation.19 | async-start | bytes 2228224 | tf_op jit(solution)/shard_map/all_gather | solution.py:83
  65.0 17.9 %copy-start.9 = (s32[2]{0:T(128)S(1)}, s32[2]{0:T(128)}, u32[]{:S(2)}) copy-start(s32[2]{0:T(128)} %constant.316) | copy-start | bytes 28
  79.3 13.8 %all-to-all-start.2 = ((bf16[16,64,256]{2,1,0:T(8,128)(2,1)}), bf16[16,64,256]{2,1,0:T(8,128)(2,1)S(1)}, u32[]{:S(2)}, u32[]{:S(2)}) async-start(bf16[16,64,256]{2,1,0:T(8,128)(2,1)} %broadcast_in_dim.89), calls=%async_computation.2 | async-start | bytes 1048576 | tf_op jit(solution)/shard_map/all_to_all | solution.py:18
  99.7 17.4 %all-to-all-start.3 = ((bf16[16,2,64,128]{3,2,1,0:T(8,128)(2,1)}), bf16[16,2,64,128]{3,2,1,0:T(8,128)(2,1)S(1)}, u32[]{:S(2)}, u32[]{:S(2)}) async-start(bf16[16,2,64,128]{3,2,1,0:T(8,128)(2,1)} %broadcast_in_dim.91), calls=%async_computation.3 | async-start | bytes 1048576 | tf_op jit(solution)/shard_map/all_to_all | solution.py:18
  118.1 13.6 %all-to-all-start.4 = ((bf16[16,64,256]{2,1,0:T(8,128)(2,1)}), bf16[16,64,256]{2,1,0:T(8,128)(2,1)S(1)}, u32[]{:S(2)}, u32[]{:S(2)}) async-start(bf16[16,64,256]{2,1,0:T(8,128)(2,1)} %broadcast_in_dim.187), calls=%async_computation.4 | async-start | bytes 1048576 | tf_op jit(solution)/shard_map/all_to_all | solution.py:18
  121.7 183.6 %all-gather.29.cloned.1.call-start = ((), (), s32[]{:S(2)}) async-start(), calls=%async_computation.20 | async-start | bytes 2228224 | tf_op jit(solution)/shard_map/all_gather | solution.py:83
  141.3 14.8 %all-to-all-start.5 = ((bf16[16,1,64,128]{3,2,1,0:T(8,128)(2,1)}), bf16[16,1,64,128]{3,2,1,0:T(8,128)(2,1)S(1)}, u32[]{:S(2)}, u32[]{:S(2)}) async-start(bf16[16,1,64,128]{3,2,1,0:T(8,128)(2,1)} %broadcast_in_dim.191), calls=%async_computation.5 | async-start | bytes 524288 | tf_op jit(solution)/shard_map/all_to_all | solution.py:18
  183.1 17.4 %all-to-all-start.7 = ((bf16[16,64,256]{2,1,0:T(8,128)(2,1)}), bf16[16,64,256]{2,1,0:T(8,128)(2,1)S(1)}, u32[]{:S(2)}, u32[]{:S(2)}) async-start(bf16[16,64,256]{2,1,0:T(8,128)(2,1)} %broadcast_in_dim.196), calls=%async_computation.7 | async-start | bytes 1048576 | tf_op jit(solution)/shard_map/all_to_all | solution.py:18
  221.6 10.2 %copy-start.5 = (bf16[6,256,128]{2,1,0:T(8,128)(2,1)S(1)}, bf16[6,256,128]{2,1,0:T(8,128)(2,1)}, u32[]{:S(2)}) copy-start(bf16[6,256,128]{2,1,0:T(8,128)(2,1)} %param.48) | copy-start | bytes 1179652
  225.3 20.2 %all-to-all-start.8 = ((bf16[16,3,64,128]{3,2,1,0:T(8,128)(2,1)}), bf16[16,3,64,128]{3,2,1,0:T(8,128)(2,1)S(1)}, u32[]{:S(2)}, u32[]{:S(2)}) async-start(bf16[16,3,64,128]{3,2,1,0:T(8,128)(2,1)} %broadcast_in_dim.197), calls=%async_computation.8 | async-start | bytes 1572864 | tf_op jit(solution)/shard_map/all_to_all | solution.py:18
  231.8 19.2 %copy-start.7 = (s32[2]{0:T(128)S(1)}, s32[2]{0:T(128)}, u32[]{:S(2)}) copy-start(s32[2]{0:T(128)} %constant.322) | copy-start | bytes 28
  246.6 13.8 %all-to-all-start.9 = ((bf16[16,64,256]{2,1,0:T(8,128)(2,1)}), bf16[16,64,256]{2,1,0:T(8,128)(2,1)S(1)}, u32[]{:S(2)}, u32[]{:S(2)}) async-start(bf16[16,64,256]{2,1,0:T(8,128)(2,1)} %broadcast_in_dim.202), calls=%async_computation.9 | async-start | bytes 1048576 | tf_op jit(solution)/shard_map/all_to_all | solution.py:18
  250.3 96.9 %all-gather.31.cloned.1.call-start = ((), (), s32[]{:S(2)}) async-start(), calls=%async_computation.21 | async-start | bytes 2228224 | tf_op jit(solution)/shard_map/all_gather | solution.py:83
  266.8 17.4 %all-to-all-start.10 = ((bf16[16,2,64,128]{3,2,1,0:T(8,128)(2,1)}), bf16[16,2,64,128]{3,2,1,0:T(8,128)(2,1)S(1)}, u32[]{:S(2)}, u32[]{:S(2)}) async-start(bf16[16,2,64,128]{3,2,1,0:T(8,128)(2,1)} %broadcast_in_dim.203), calls=%async_computation.10 | async-start | bytes 1048576 | tf_op jit(solution)/shard_map/all_to_all | solution.py:18
  308.5 14.7 %all-to-all-start.12 = ((bf16[16,1,64,128]{3,2,1,0:T(8,128)(2,1)}), bf16[16,1,64,128]{3,2,1,0:T(8,128)(2,1)S(1)}, u32[]{:S(2)}, u32[]{:S(2)}) async-start(bf16[16,1,64,128]{3,2,1,0:T(8,128)(2,1)} %broadcast_in_dim.210), calls=%async_computation.12 | async-start | bytes 524288 | tf_op jit(solution)/shard_map/all_to_all | solution.py:18
  (6 other events, 51.4 us)
Sparse Core Ops, SparseCore 0:
  9.1 45.1 all-gather.16
  56.0 40.1 all-gather.18
  98.0 40.0 all-gather.20
  139.7 40.0 all-gather.22
  181.4 40.1 all-gather.24
  223.2 40.1 all-gather.26
  265.1 40.0 all-gather.28
  307.0 40.0 all-gather.30
where the time goes:
time: 359 us; the launch traced here: 357 us
  waiting for transfers between devices  195 us (54%)
  starting transfers between devices  64.4 us (18%)
  blocking collectives  39 us (11%)
  local copies, waits for them, and re-layouts  21.9 us (6%)
  matrix products  20.8 us (6%)
  between operations  14.5 us (4%)
    all_to_all x11, waiting for transfers between devices, from_everyone(): lax.all_to_all(jnp.broadcast_to(value[None], (length, *value.shape)), axi...  106 us
    all_to_all x11, starting transfers between devices, from_everyone(): lax.all_to_all(jnp.broadcast_to(value[None], (length, *value.shape)), axi...  64.1 us
    all_gather x4, waiting for transfers between devices, shards(): lax.all_gather(inv_lower[section], 'row', axis=1, tiled=True)  42.8 us
    all_gather x4, waiting for transfers between devices, shards(): lax.all_gather(inv_upper[section], 'row', axis=1, tiled=True)  42.2 us
    all_to_all x3, blocking collectives, from_everyone(): lax.all_to_all(jnp.broadcast_to(value[None], (length, *value.shape)), axi...  39 us
    dot_general x8, matrix products, times_inverse(): lax.dot_general(block, inverse, (((1,), (1,)), ((), ())), preferred_eleme...  18.9 us
    broadcast_in_dim x19, local copies, waits for them, and re-layouts, from_everyone(): jnp.broadcast_to(value[None], (length, *value.shape))  9.98 us
  transfers between devices with their start and end apart: 19, of which 19 were waited for; matrix products, arithmetic and copies ran while one was open for 11% of the time, Pallas kernels for 0%

commit v1 on v0

--- a/solution.py
+++ b/solution.py
@@ -54,7 +54,14 @@
     for section in range(tile_count):
         rounded = residual[section].astype(jnp.bfloat16)
         whole = gathered_copies(rounded, "col", 1)
-        solved = fold_columns(whole, lax.all_gather(inv_lower[section], "row", axis=1, tiled=True))
+
+        def enter_strings(v0, dimension_no):
+            return jnp.concatenate(
+                lax.all_to_all(jnp.stack(lax.psum(1, axis_name="row") * [v0], 0), "row", 0, 0),
+                axis=dimension_no,
+            )
+
+        solved = fold_columns(whole, enter_strings(inv_lower[section], 1))
         forward.append(solved)
         if section + 1 < tile_count:
             pair_index = np.array(

time: 359 us -> 480 us (1.34); the launches traced: 357 us -> 470 us
  waiting for transfers between devices: 195 us -> 263 us
  blocking collectives: 39 us -> 78.6 us
  local copies, waits for them, and re-layouts: 21.9 us -> 29.7 us
    all_to_all x0 -> x4, waiting for transfers between devices: none -> 191 us  [enter_strings(): lax.all_to_all(jnp.stack(lax.psum(1, axis_name='row') * [v0], 0), 'row',...]
    all_gather x4 -> x0, waiting for transfers between devices: 42.8 us -> none  [shards(): lax.all_gather(inv_lower[section], 'row', axis=1, tiled=True)]
    all_gather x4, waiting for transfers between devices: 42.2 us -> 0.08 us  [shards(): lax.all_gather(inv_upper[section], 'row', axis=1, tiled=True)]
    all_to_all x3 -> x6, blocking collectives: 39 us -> 78.6 us  [from_everyone(): lax.all_to_all(jnp.broadcast_to(value[None], (length, *value.shape)), axi...]
    all_to_all x11 -> x8, waiting for transfers between devices: 106 us -> 70.5 us  [from_everyone(): lax.all_to_all(jnp.broadcast_to(value[None], (length, *value.shape)), axi...]
    all_to_all x0 -> x4, starting transfers between devices: none -> 33.5 us  [enter_strings(): lax.all_to_all(jnp.stack(lax.psum(1, axis_name='row') * [v0], 0), 'row',...]
    all_to_all x11 -> x8, starting transfers between devices: 64.1 us -> 32.6 us  [from_everyone(): lax.all_to_all(jnp.broadcast_to(value[None], (length, *value.shape)), axi...]
    dot_general x8, matrix products: 18.9 us -> 12.5 us  [times_inverse(): lax.dot_general(block, inverse, (((1,), (1,)), ((), ())), preferred_eleme...]
  transfers between devices with their start and end apart: 19 -> 16, of which waited for: 19 -> 12; matrix products, arithmetic and copies ran while one was open for 11% -> 8% of each run, Pallas kernels for 0% -> 0%
where the time goes in v1:
time: 480 us; the launch traced here: 470 us
  waiting for transfers between devices  263 us (55%)
  blocking collectives  78.6 us (16%)
  starting transfers between devices  66.2 us (14%)
  local copies, waits for them, and re-layouts  29.7 us (6%)
  matrix products  17 us (4%)
  between operations  14.3 us (3%)
    all_to_all x4, waiting for transfers between devices, enter_strings(): lax.all_to_all(jnp.stack(lax.psum(1, axis_name='row') * [v0], 0), 'row',...  191 us
    all_to_all x6, blocking collectives, from_everyone(): lax.all_to_all(jnp.broadcast_to(value[None], (length, *value.shape)), axi...  78.6 us
    all_to_all x8, waiting for transfers between devices, from_everyone(): lax.all_to_all(jnp.broadcast_to(value[None], (length, *value.shape)), axi...  70.5 us
    all_to_all x4, starting transfers between devices, enter_strings(): lax.all_to_all(jnp.stack(lax.psum(1, axis_name='row') * [v0], 0), 'row',...  33.5 us
    all_to_all x8, starting transfers between devices, from_everyone(): lax.all_to_all(jnp.broadcast_to(value[None], (length, *value.shape)), axi...  32.6 us
    dot_general x8, matrix products, times_inverse(): lax.dot_general(block, inverse, (((1,), (1,)), ((), ())), preferred_eleme...  12.5 us
  transfers between devices with their start and end apart: 16, of which 12 were waited for; matrix products, arithmetic and copies ran while one was open for 8% of the time, Pallas kernels for 0%

profile of v1, /device:TPU:1, one launch (start us, length us, event | category | flops | bytes accessed | tf_op | source)
XLA Modules:
  0.0 470.5 jit_solution(17576627437974224374)
XLA Ops:
  8.2 7.6 %all-to-all-start = ((bf16[16,64,256]{2,1,0:T(8,128)(2,1)}), bf16[16,64,256]{2,1,0:T(8,128)(2,1)S(1)}, u32[]{:S(2)}, u32[]{:S(2)}) async-start(bf16[16,64,256]{2,1,0:T(8,128)(2,1)} %broadcast_in_dim.83), calls=%async_computation | async-start | bytes 1048576 | tf_op jit(solution)/shard_map/all_to_all | solution.py:18
  17.0 9.4 %all-to-all-done = bf16[16,64,256]{2,1,0:T(8,128)(2,1)S(1)} async-done(((bf16[16,64,256]{2,1,0:T(8,128)(2,1)}), bf16[16,64,256]{2,1,0:T(8,128)(2,1)S(1)}, u32[]{:S(2)}, u32[]{:S(2)}) %all-to-all-start) | async-done | bytes 524320 | tf_op jit(solution)/shard_map/all_to_all | solution.py:18
  27.9 10.6 %all-to-all-start.1 = ((bf16[16,256,256]{2,1,0:T(8,128)(2,1)}), bf16[16,256,256]{2,1,0:T(8,128)(2,1)S(1)}, u32[]{:S(2)}, u32[]{:S(2)}) async-start(bf16[16,256,256]{2,1,0:T(8,128)(2,1)} %stack.40), calls=%async_computation.1 | async-start | bytes 4194304 | tf_op jit(solution)/shard_map/all_to_all | solution.py:60
  40.1 47.3 %all-to-all-done.1 = bf16[16,256,256]{2,1,0:T(8,128)(2,1)S(1)} async-done(((bf16[16,256,256]{2,1,0:T(8,128)(2,1)}), bf16[16,256,256]{2,1,0:T(8,128)(2,1)S(1)}, u32[]{:S(2)}, u32[]{:S(2)}) %all-to-all-start.1) | async-done | bytes 2097184 | tf_op jit(solution)/shard_map/all_to_all | solution.py:60
  88.5 16.5 %all_to_all.90 = bf16[16,3,64,128]{3,2,1,0:T(8,128)(2,1)S(1)} all-to-all(bf16[16,3,64,128]{3,2,1,0:T(8,128)(2,1)S(1)} %broadcast_in_dim.85), channel_id=1, replica_groups=mesh['row'=16,'col'=16] {'col'}, dimensions={0} | all-to-all | bytes 1572864 | tf_op jit(solution)/shard_map/all_to_all | solution.py:18
  106.6 6.1 %all-to-all-start.4 = ((bf16[16,256,256]{2,1,0:T(8,128)(2,1)}), bf16[16,256,256]{2,1,0:T(8,128)(2,1)S(1)}, u32[]{:S(2)}, u32[]{:S(2)}) async-start(bf16[16,256,256]{2,1,0:T(8,128)(2,1)} %stack.42), calls=%async_computation.4 | async-start | bytes 4194304 | tf_op jit(solution)/shard_map/all_to_all | solution.py:60
  116.4 45.3 %all-to-all-done.4 = bf16[16,256,256]{2,1,0:T(8,128)(2,1)S(1)} async-done(((bf16[16,256,256]{2,1,0:T(8,128)(2,1)}), bf16[16,256,256]{2,1,0:T(8,128)(2,1)S(1)}, u32[]{:S(2)}, u32[]{:S(2)}) %all-to-all-start.4) | async-done | bytes 2097184 | tf_op jit(solution)/shard_map/all_to_all | solution.py:60
  167.8 9.4 %all-to-all-done.3 = bf16[16,64,256]{2,1,0:T(8,128)(2,1)S(1)} async-done(((bf16[16,64,256]{2,1,0:T(8,128)(2,1)}), bf16[16,64,256]{2,1,0:T(8,128)(2,1)S(1)}, u32[]{:S(2)}, u32[]{:S(2)}) %all-to-all-start.3) | async-done | bytes 524320 | tf_op jit(solution)/shard_map/all_to_all | solution.py:18
  178.2 13.4 %all_to_all.91 = bf16[16,2,64,128]{3,2,1,0:T(8,128)(2,1)S(1)} all-to-all(bf16[16,2,64,128]{3,2,1,0:T(8,128)(2,1)S(1)} %broadcast_in_dim.91), channel_id=1, replica_groups=mesh['row'=16,'col'=16] {'col'}, dimensions={0} | all-to-all | bytes 1048576 | tf_op jit(solution)/shard_map/all_to_all | solution.py:18
  193.1 6.7 %all-to-all-start.7 = ((bf16[16,256,256]{2,1,0:T(8,128)(2,1)}), bf16[16,256,256]{2,1,0:T(8,128)(2,1)S(1)}, u32[]{:S(2)}, u32[]{:S(2)}) async-start(bf16[16,256,256]{2,1,0:T(8,128)(2,1)} %stack.44), calls=%async_computation.7 | async-start | bytes 4194304 | tf_op jit(solution)/shard_map/all_to_all | solution.py:60
  204.3 50.0 %all-to-all-done.7 = bf16[16,256,256]{2,1,0:T(8,128)(2,1)S(1)} async-done(((bf16[16,256,256]{2,1,0:T(8,128)(2,1)}), bf16[16,256,256]{2,1,0:T(8,128)(2,1)S(1)}, u32[]{:S(2)}, u32[]{:S(2)}) %all-to-all-start.7) | async-done | bytes 2097184 | tf_op jit(solution)/shard_map/all_to_all | solution.py:60
  259.5 9.1 %all-to-all-done.6 = bf16[16,64,256]{2,1,0:T(8,128)(2,1)S(1)} async-done(((bf16[16,64,256]{2,1,0:T(8,128)(2,1)}), bf16[16,64,256]{2,1,0:T(8,128)(2,1)S(1)}, u32[]{:S(2)}, u32[]{:S(2)}) %all-to-all-start.6) | async-done | bytes 524320 | tf_op jit(solution)/shard_map/all_to_all | solution.py:18
  270.4 10.5 %all_to_all.92 = bf16[16,1,64,128]{3,2,1,0:T(8,128)(2,1)S(1)} all-to-all(bf16[16,1,64,128]{3,2,1,0:T(8,128)(2,1)S(1)} %broadcast_in_dim.191), channel_id=1, replica_groups=mesh['row'=16,'col'=16] {'col'}, dimensions={0} | all-to-all | bytes 524288 | tf_op jit(solution)/shard_map/all_to_all | solution.py:18
  282.5 10.1 %all-to-all-start.10 = ((bf16[16,256,256]{2,1,0:T(8,128)(2,1)}), bf16[16,256,256]{2,1,0:T(8,128)(2,1)S(1)}, u32[]{:S(2)}, u32[]{:S(2)}) async-start(bf16[16,256,256]{2,1,0:T(8,128)(2,1)} %stack.47), calls=%async_computation.10 | async-start | bytes 4194304 | tf_op jit(solution)/shard_map/all_to_all | solution.py:60
  295.6 48.0 %all-to-all-done.10 = bf16[16,256,256]{2,1,0:T(8,128)(2,1)S(1)} async-done(((bf16[16,256,256]{2,1,0:T(8,128)(2,1)}), bf16[16,256,256]{2,1,0:T(8,128)(2,1)S(1)}, u32[]{:S(2)}, u32[]{:S(2)}) %all-to-all-start.10) | async-done | bytes 2097184 | tf_op jit(solution)/shard_map/all_to_all | solution.py:60
  343.6 15.0 %all_to_all.93 = bf16[16,64,256]{2,1,0:T(8,128)(2,1)S(1)} all-to-all(bf16[16,64,256]{2,1,0:T(8,128)(2,1)S(1)} %broadcast_in_dim.195), channel_id=1, replica_groups=mesh['row'=16,'col'=16] {'col'}, dimensions={0} | all-to-all | bytes 1048576 | tf_op jit(solution)/shard_map/all_to_all | solution.py:18
  364.4 9.1 %all-to-all-done.11 = bf16[16,64,256]{2,1,0:T(8,128)(2,1)S(1)} async-done(((bf16[16,64,256]{2,1,0:T(8,128)(2,1)}), bf16[16,64,256]{2,1,0:T(8,128)(2,1)S(1)}, u32[]{:S(2)}, u32[]{:S(2)}) %all-to-all-start.11) | async-done | bytes 524320 | tf_op jit(solution)/shard_map/all_to_all | solution.py:18
  377.3 3.6 all-to-all-start.12
  382.2 10.4 %all-to-all-done.12 = bf16[16,3,64,128]{3,2,1,0:T(8,128)(2,1)S(1)} async-done(((bf16[16,3,64,128]{3,2,1,0:T(8,128)(2,1)}), bf16[16,3,64,128]{3,2,1,0:T(8,128)(2,1)S(1)}, u32[]{:S(2)}, u32[]{:S(2)}) %all-to-all-start.12) | async-done | bytes 786464 | tf_op jit(solution)/shard_map/all_to_all | solution.py:18
  398.6 7.9 %all-to-all-done.13 = bf16[16,64,256]{2,1,0:T(8,128)(2,1)S(1)} async-done(((bf16[16,64,256]{2,1,0:T(8,128)(2,1)}), bf16[16,64,256]{2,1,0:T(8,128)(2,1)S(1)}, u32[]{:S(2)}, u32[]{:S(2)}) %all-to-all-start.13) | async-done | bytes 524320 | tf_op jit(solution)/shard_map/all_to_all | solution.py:18
  414.9 7.7 %all-to-all-done.14 = bf16[16,2,64,128]{3,2,1,0:T(8,128)(2,1)S(1)} async-done(((bf16[16,2,64,128]{3,2,1,0:T(8,128)(2,1)}), bf16[16,2,64,128]{3,2,1,0:T(8,128)(2,1)S(1)}, u32[]{:S(2)}, u32[]{:S(2)}) %all-to-all-start.14) | async-done | bytes 524320 | tf_op jit(solution)/shard_map/all_to_all | solution.py:18
  422.9 11.6 %all_to_all.94 = bf16[16,64,256]{2,1,0:T(8,128)(2,1)S(1)} all-to-all(bf16[16,64,256]{2,1,0:T(8,128)(2,1)S(1)} %broadcast_in_dim.208), channel_id=1, replica_groups=mesh['row'=16,'col'=16] {'col'}, dimensions={0} | all-to-all | bytes 1048576 | tf_op jit(solution)/shard_map/all_to_all | solution.py:18
  441.5 7.5 %all-to-all-done.16 = bf16[16,1,64,128]{3,2,1,0:T(8,128)(2,1)S(1)} async-done(((bf16[16,1,64,128]{3,2,1,0:T(8,128)(2,1)}), bf16[16,1,64,128]{3,2,1,0:T(8,128)(2,1)S(1)}, u32[]{:S(2)}, u32[]{:S(2)}) %all-to-all-start.16) | async-done | bytes 262176 | tf_op jit(solution)/shard_map/all_to_all | solution.py:18
  449.2 11.6 %all_to_all.95 = bf16[16,64,256]{2,1,0:T(8,128)(2,1)S(1)} all-to-all(bf16[16,64,256]{2,1,0:T(8,128)(2,1)S(1)} %broadcast_in_dim.214), channel_id=1, replica_groups=mesh['row'=16,'col'=16] {'col'}, dimensions={0} | all-to-all | bytes 1048576 | tf_op jit(solution)/shard_map/all_to_all | solution.py:18
  (117 shorter events, 71.8 us)
Async XLA Ops:
  8.2 18.1 %all-to-all-start = ((bf16[16,64,256]{2,1,0:T(8,128)(2,1)}), bf16[16,64,256]{2,1,0:T(8,128)(2,1)S(1)}, u32[]{:S(2)}, u32[]{:S(2)}) async-start(bf16[16,64,256]{2,1,0:T(8,128)(2,1)} %broadcast_in_dim.83), calls=%async_computation | async-start | bytes 1048576 | tf_op jit(solution)/shard_map/all_to_all | solution.py:18
  27.9 10.6 %copy-start.7 = (s32[3]{0:T(128)S(1)}, s32[3]{0:T(128)}, u32[]{:S(2)}) copy-start(s32[3]{0:T(128)} %constant.313) | copy-start | bytes 40
  27.9 59.5 %all-to-all-start.1 = ((bf16[16,256,256]{2,1,0:T(8,128)(2,1)}), bf16[16,256,256]{2,1,0:T(8,128)(2,1)S(1)}, u32[]{:S(2)}, u32[]{:S(2)}) async-start(bf16[16,256,256]{2,1,0:T(8,128)(2,1)} %stack.40), calls=%async_computation.1 | async-start | bytes 4194304 | tf_op jit(solution)/shard_map/all_to_all | solution.py:60
  106.6 7.7 %copy-start = (s32[6]{0:T(128)S(1)}, s32[6]{0:T(128)}, u32[]{:S(2)}) copy-start(s32[6]{0:T(128)} %param.50) | copy-start | bytes 76
  106.6 55.1 %all-to-all-start.4 = ((bf16[16,256,256]{2,1,0:T(8,128)(2,1)}), bf16[16,256,256]{2,1,0:T(8,128)(2,1)S(1)}, u32[]{:S(2)}, u32[]{:S(2)}) async-start(bf16[16,256,256]{2,1,0:T(8,128)(2,1)} %stack.42), calls=%async_computation.4 | async-start | bytes 4194304 | tf_op jit(solution)/shard_map/all_to_all | solution.py:60
  112.8 53.4 %copy-start.6 = (s32[2]{0:T(128)S(1)}, s32[2]{0:T(128)}, u32[]{:S(2)}) copy-start(s32[2]{0:T(128)} %constant.316) | copy-start | bytes 28
  162.6 14.6 %all-to-all-start.3 = ((bf16[16,64,256]{2,1,0:T(8,128)(2,1)}), bf16[16,64,256]{2,1,0:T(8,128)(2,1)S(1)}, u32[]{:S(2)}, u32[]{:S(2)}) async-start(bf16[16,64,256]{2,1,0:T(8,128)(2,1)} %broadcast_in_dim.89), calls=%async_computation.3 | async-start | bytes 1048576 | tf_op jit(solution)/shard_map/all_to_all | solution.py:18
  193.1 61.2 %all-to-all-start.7 = ((bf16[16,256,256]{2,1,0:T(8,128)(2,1)}), bf16[16,256,256]{2,1,0:T(8,128)(2,1)S(1)}, u32[]{:S(2)}, u32[]{:S(2)}) async-start(bf16[16,256,256]{2,1,0:T(8,128)(2,1)} %stack.44), calls=%async_computation.7 | async-start | bytes 4194304 | tf_op jit(solution)/shard_map/all_to_all | solution.py:60
  199.8 173.8 %all-gather.9.cloned.1.call-start = ((), (), s32[]{:S(2)}) async-start(), calls=%async_computation.18 | async-start | bytes 2228224 | tf_op jit(solution)/shard_map/all_gather | solution.py:90
  255.1 13.5 %all-to-all-start.6 = ((bf16[16,64,256]{2,1,0:T(8,128)(2,1)}), bf16[16,64,256]{2,1,0:T(8,128)(2,1)S(1)}, u32[]{:S(2)}, u32[]{:S(2)}) async-start(bf16[16,64,256]{2,1,0:T(8,128)(2,1)} %broadcast_in_dim.187), calls=%async_computation.6 | async-start | bytes 1048576 | tf_op jit(solution)/shard_map/all_to_all | solution.py:18
  258.7 147.8 %all-gather.11.cloned.1.call-start = ((), (), s32[]{:S(2)}) async-start(), calls=%async_computation.19 | async-start | bytes 2228224 | tf_op jit(solution)/shard_map/all_gather | solution.py:90
  282.5 61.1 %all-to-all-start.10 = ((bf16[16,256,256]{2,1,0:T(8,128)(2,1)}), bf16[16,256,256]{2,1,0:T(8,128)(2,1)S(1)}, u32[]{:S(2)}, u32[]{:S(2)}) async-start(bf16[16,256,256]{2,1,0:T(8,128)(2,1)} %stack.47), calls=%async_computation.10 | async-start | bytes 4194304 | tf_op jit(solution)/shard_map/all_to_all | solution.py:60
  292.6 142.0 %all-gather.13.cloned.1.call-start = ((), (), s32[]{:S(2)}) async-start(), calls=%async_computation.20 | async-start | bytes 2228224 | tf_op jit(solution)/shard_map/all_gather | solution.py:90
  358.6 5.2 %copy-start.5 = (s32[3]{0:T(128)S(1)}, s32[3]{0:T(128)}, u32[]{:S(2)}) copy-start(s32[3]{0:T(128)} %constant.319) | copy-start | bytes 40
  358.6 5.2 %copy-start.2 = (bf16[6,256,128]{2,1,0:T(8,128)(2,1)S(1)}, bf16[6,256,128]{2,1,0:T(8,128)(2,1)}, u32[]{:S(2)}) copy-start(bf16[6,256,128]{2,1,0:T(8,128)(2,1)} %param.49) | copy-start | bytes 1179652
  360.2 13.3 %all-to-all-start.11 = ((bf16[16,64,256]{2,1,0:T(8,128)(2,1)}), bf16[16,64,256]{2,1,0:T(8,128)(2,1)S(1)}, u32[]{:S(2)}, u32[]{:S(2)}) async-start(bf16[16,64,256]{2,1,0:T(8,128)(2,1)} %broadcast_in_dim.196), calls=%async_computation.11 | async-start | bytes 1048576 | tf_op jit(solution)/shard_map/all_to_all | solution.py:18
  373.6 7.3 %copy-start.3 = (bf16[6,256,128]{2,1,0:T(8,128)(2,1)S(1)}, bf16[6,256,128]{2,1,0:T(8,128)(2,1)}, u32[]{:S(2)}) copy-start(bf16[6,256,128]{2,1,0:T(8,128)(2,1)} %param.48) | copy-start | bytes 1179652
  376.0 5.5 %copy-start.1 = (s32[6]{0:T(128)S(1)}, s32[6]{0:T(128)}, u32[]{:S(2)}) copy-start(s32[6]{0:T(128)} %param.51) | copy-start | bytes 76
  377.3 15.3 %all-to-all-start.12 = ((bf16[16,3,64,128]{3,2,1,0:T(8,128)(2,1)}), bf16[16,3,64,128]{3,2,1,0:T(8,128)(2,1)S(1)}, u32[]{:S(2)}, u32[]{:S(2)}) async-start(bf16[16,3,64,128]{3,2,1,0:T(8,128)(2,1)} %broadcast_in_dim.197), calls=%async_computation.12 | async-start | bytes 1572864 | tf_op jit(solution)/shard_map/all_to_all | solution.py:18
  380.9 17.1 %copy-start.4 = (s32[2]{0:T(128)S(1)}, s32[2]{0:T(128)}, u32[]{:S(2)}) copy-start(s32[2]{0:T(128)} %constant.322) | copy-start | bytes 28
  393.8 12.7 %all-to-all-start.13 = ((bf16[16,64,256]{2,1,0:T(8,128)(2,1)}), bf16[16,64,256]{2,1,0:T(8,128)(2,1)S(1)}, u32[]{:S(2)}, u32[]{:S(2)}) async-start(bf16[16,64,256]{2,1,0:T(8,128)(2,1)} %broadcast_in_dim.202), calls=%async_computation.13 | async-start | bytes 1048576 | tf_op jit(solution)/shard_map/all_to_all | solution.py:18
  397.4 63.5 %all-gather.15.cloned.1.call-start = ((), (), s32[]{:S(2)}) async-start(), calls=%async_computation.21 | async-start | bytes 2228224 | tf_op jit(solution)/shard_map/all_gather | solution.py:90
  410.0 12.5 %all-to-all-start.14 = ((bf16[16,2,64,128]{3,2,1,0:T(8,128)(2,1)}), bf16[16,2,64,128]{3,2,1,0:T(8,128)(2,1)S(1)}, u32[]{:S(2)}, u32[]{:S(2)}) async-start(bf16[16,2,64,128]{3,2,1,0:T(8,128)(2,1)} %broadcast_in_dim.203), calls=%async_computation.14 | async-start | bytes 1048576 | tf_op jit(solution)/shard_map/all_to_all | solution.py:18
  437.9 11.0 %all-to-all-start.16 = ((bf16[16,1,64,128]{3,2,1,0:T(8,128)(2,1)}), bf16[16,1,64,128]{3,2,1,0:T(8,128)(2,1)S(1)}, u32[]{:S(2)}, u32[]{:S(2)}) async-start(bf16[16,1,64,128]{3,2,1,0:T(8,128)(2,1)} %broadcast_in_dim.210), calls=%async_computation.16 | async-start | bytes 524288 | tf_op jit(solution)/shard_map/all_to_all | solution.py:18
Sparse Core Ops, SparseCore 0:
  202.3 62.9 all-gather.8
  267.1 54.5 all-gather.10
  323.5 49.5 all-gather.12
  399.7 43.4 all-gather.14
